TPU v7x, 128 devices: a whole 4x4x4 slice. The times are simulated.
128 devices in a mesh: tgt: 16 (over z, x), src: 8 (over y, core).
Axes of the slice: x: 4, y: 4, z: 4, core: 2. Of those that a mesh axis runs over, the one named last changes fastest.
Arguments:
- points: bfloat16 [262144, 256], P(('tgt', 'src')), may hold values from -0.4 to 0.4
- weights: bfloat16 [262144, 64], P(('tgt', 'src')), may hold values from -6 to 6
- near_list: int32 [2048, 16], P(('tgt', 'src')), may hold values from -1 to 127, as said below
- far_list: int32 [2048, 3, 8], P('tgt', None, 'src'), may hold values from -1 to 63, as said below
- skel_index: int32 [896, 256], P(('tgt', 'src')), may hold values from 0 to 2047, as said below
- equiv_weights: bfloat16 [896, 256, 64], P(('tgt', 'src')), may hold values from -6 to 6
Outputs:
- potential: float32 [262144, 64], P(('tgt', 'src'))
Inputs may be any that keep to these rules, and one draw needn't show every extreme that they name: `near_list`: row b lists blocks of b's group of 128 blocks by their index within the group: first b itself, then distinct other blocks; after a row's live entries all are -1; every row has 4 or more live entries. `far_list`: entry [b, l, c] is -1 or a level-l node owned by a device of src index c, numbered as the owner's tgt index times (16 // (4 * 2 ** l)) plus the node's number among the owner's level-l nodes. `skel_index`: Level-l nodes of a device cover 4 * 128 * 2 ** l consecutive points of that device each, in order; a node's 256 entries are increasing indices of the device's points inside the node.
All inputs are finite; a program needn't handle non-finite values.
Results may differ from a plain program's by a relative error of at most 0.0023.
Values may be sent and summed in bfloat16 or wider, within the bound.
No kernel may reach another device: no remote copies, remote signals or barrier semaphores. Data moves between devices by JAX's collectives and lax.ppermute only.
A program may use at most 192 MiB of HBM per device.

v0:
```python
import jax
import jax.numpy as jnp
from jax import lax
from jax.sharding import PartitionSpec as P

E = 256
WCOL = 64
BLK = 128
RANK = 256
NEAR = 16
LEVELS = 3
kernel_rate = 2.0


def square_norms(values):
    return jnp.sum(jnp.square(values.astype(jnp.float32)), axis=-1)


def tile_kernel(targets, target_norms, sources, source_norms, live_mask):
    dot_terms = jnp.einsum("bie,bse->bis", targets, sources, preferred_element_type=jnp.float32)
    sq_dist = target_norms[:, :, None] + source_norms[:, None, :] - 2.0 * dot_terms
    return jnp.where(live_mask[:, None, :], jnp.exp(-kernel_rate * sq_dist), 0.0).astype(
        jnp.bfloat16
    )


def apply_tile(kernel, source_weights):
    return jnp.einsum("bis,bsw->biw", kernel, source_weights, preferred_element_type=jnp.float32)


def shards(points, weights, near_list, far_list, skel_index, equiv_weights):
    point_dev = points.shape[0]
    blk_dev = point_dev // BLK
    src_size = lax.axis_size("src")
    src_index = lax.axis_index("src")
    group_blocks = src_size * blk_dev
    node_dev = skel_index.shape[0]
    level_nodes = [blk_dev // (4 * 2**tree_level) for tree_level in range(LEVELS)]
    level_start = [sum(level_nodes[:tree_level]) for tree_level in range(LEVELS)]
    group_pts, group_wts = (
        lax.all_gather(points, "src", axis=0, tiled=True),
        lax.all_gather(weights, "src", axis=0, tiled=True),
    )
    tgt_blocks = group_pts.reshape(group_blocks, BLK, E)
    tgt_norms = square_norms(group_pts).reshape(group_blocks, BLK)
    wt_blocks = group_wts.reshape(group_blocks, BLK, WCOL)
    skel_pts = jnp.take(points, skel_index.reshape(-1), axis=0).reshape(node_dev, RANK, E)
    panels = []
    for tree_level in range(LEVELS):
        first_node = level_start[tree_level]
        last_node = first_node + level_nodes[tree_level]
        lvl_pts, lvl_wts = (
            lax.all_gather(skel_pts[first_node:last_node], "tgt", axis=0, tiled=True),
            lax.all_gather(equiv_weights[first_node:last_node], "tgt", axis=0, tiled=True),
        )
        panels.append((lvl_pts, square_norms(lvl_pts), lvl_wts, level_nodes[tree_level], 0))
    own_blocks = points.reshape(blk_dev, BLK, E)
    own_norms = lax.dynamic_slice_in_dim(tgt_norms, src_index * blk_dev, blk_dev, 0)
    near_live = near_list >= 0
    near_index = jnp.where(near_live, near_list, 0)
    sources = tgt_blocks[near_index].reshape(blk_dev, NEAR * BLK, E)
    source_norms = tgt_norms[near_index].reshape(blk_dev, NEAR * BLK)
    source_wts = wt_blocks[near_index].reshape(blk_dev, NEAR * BLK, WCOL)
    kernel = tile_kernel(
        own_blocks, own_norms, sources, source_norms, jnp.repeat(near_live, BLK, axis=1)
    )
    own_near = apply_tile(kernel, source_wts).reshape(point_dev, WCOL)
    row_count = src_size * point_dev
    block_count = row_count // BLK
    far_total = jnp.zeros((block_count, BLK, WCOL), jnp.float32)
    for tree_level in range(LEVELS):
        panel_pts, panel_norms, panel_wts, stride_rows, offset_rows = panels[tree_level]
        level_count = level_nodes[tree_level]
        far_entry = far_list[:, tree_level, 0]
        far_live = far_entry >= 0
        far_entry = jnp.where(far_live, far_entry, 0)
        panel_rows = far_entry // level_count * stride_rows + offset_rows + far_entry % level_count
        kernel = tile_kernel(
            tgt_blocks,
            tgt_norms,
            panel_pts[panel_rows],
            panel_norms[panel_rows],
            jnp.broadcast_to(far_live[:, None], (block_count, RANK)),
        )
        far_total = far_total + apply_tile(kernel, panel_wts[panel_rows])
    whole_term = lax.psum(far_total.reshape(row_count, WCOL), "src")
    mine_term = lax.dynamic_slice_in_dim(whole_term, src_index * point_dev, point_dev, 0)
    mine_term = mine_term + own_near
    return mine_term


def solution(mesh):
    in_specs = (
        P(("tgt", "src"), None),
        P(("tgt", "src"), None),
        P(("tgt", "src"), None),
        P("tgt", None, "src"),
        P(("tgt", "src"), None),
        P(("tgt", "src"), None, None),
    )
    out_specs = P(("tgt", "src"), None)
    return jax.shard_map(shards, mesh=mesh, in_specs=in_specs, out_specs=out_specs, check_vma=False)
```

profile of v0, /device:TPU:0, one launch (start us, length us, event | category | flops | bytes accessed | tf_op | source)
XLA Modules:
  0.0 471.0 jit_solution(658145759099932878)
XLA Ops:
  10.4 5.5 %gather_fusion = bf16[1792,256]{1,0:T(8,128)(2,1)S(1)} fusion(bf16[2048,256]{1,0:T(8,128)(2,1)} %param.6, s32[2048]{0:T(1024)S(1)} %pad_clamp_fusion), kind=kCustom, calls=%fused_computation | custom fusion | bytes 1842176 | tf_op jit(solution)/shard_map/jit(_take)/gather | solution.py:47
  20.4 26.1 %all_gather.30 = bf16[16,256,64]{1,2,0:T(8,128)(2,1)S(1)} all-gather(bf16[1,256,64]{1,2,0:T(8,128)(2,1)S(1)} %slice-done), channel_id=1, replica_groups=mesh['tgt'=16,'src'=8] {'tgt'}, dimensions={0}, use_global_device_ids=true | all-gather | bytes 557056 | tf_op jit(solution)/shard_map/all_gather | solution.py:54
  49.3 5.6 %all-gather.17.cloned.1.call-done = bf16[32,256,64]{1,2,0:T(8,128)(2,1)} async-done(((bf16[2,256,64]{1,2,0:T(8,128)(2,1)}), bf16[32,256,64]{1,2,0:T(8,128)(2,1)}) %all-gather.17.cloned.1.call-update) | async-done | bytes 1048592 | tf_op jit(solution)/shard_map/all_gather | solution.py:54
  58.9 22.5 %all-gather.19.cloned.1.call-done = bf16[16384,64]{0,1:T(8,128)(2,1)} async-done(((bf16[2048,64]{0,1:T(8,128)(2,1)}), bf16[16384,64]{0,1:T(8,128)(2,1)}) %all-gather.19.cloned.1.call-update) | async-done | bytes 2097168 | tf_op jit(solution)/shard_map/all_gather | solution.py:42
  86.7 6.9 %copy.25 = bf16[256,128,64]{1,0,2:T(8,128)(2,1)} copy(bf16[256,128,64]{1,2,0:T(8,128)(2,1)} %gather_fusion.12) | data formatting | bytes 8388608 | tf_op jit(solution)/shard_map/gather | solution.py:63
  93.6 7.3 %reshape.311 = bf16[16,2048,64]{1,0,2:T(8,128)(2,1)} reshape(bf16[256,128,64]{1,0,2:T(8,128)(2,1)} %copy.25) | data formatting | bytes 8388608 | tf_op jit(solution)/shard_map/reshape | solution.py:63
  100.9 28.0 %all-gather.21.cloned.1.call-done = bf16[4096,256]{1,0:T(8,128)(2,1)} async-done(((bf16[256,256]{1,0:T(8,128)(2,1)}), bf16[4096,256]{1,0:T(8,128)(2,1)}) %all-gather.21.cloned.1.call-update) | async-done | bytes 2097168 | tf_op jit(solution)/shard_map/all_gather | solution.py:53
  128.9 10.0 %gather_fusion.8 = bf16[128,256,256]{2,1,0:T(8,128)(2,1)} fusion(bf16[16,256,256]{2,1,0:T(8,128)(2,1)} %bitcast.126, s32[1024]{0:T(1024)S(1)} %pad_clamp_fusion.2), kind=kCustom, calls=%fused_computation.8 | custom fusion | bytes 33554944 | tf_op jit(solution)/shard_map/gather | solution.py:81
  140.3 34.9 %all-gather.13.cloned.1.call-done = bf16[64,256,64]{1,2,0:T(8,128)(2,1)} async-done(((bf16[4,256,64]{1,2,0:T(8,128)(2,1)}), bf16[64,256,64]{1,2,0:T(8,128)(2,1)}) %all-gather.13.cloned.1.call-update) | async-done | bytes 2097168 | tf_op jit(solution)/shard_map/all_gather | solution.py:54
  179.6 48.4 %all-gather.15.cloned.1.call-done = bf16[32,256,256]{2,1,0:T(8,128)(2,1)} async-done(((bf16[2,256,256]{2,1,0:T(8,128)(2,1)}), bf16[32,256,256]{2,1,0:T(8,128)(2,1)}) %all-gather.15.cloned.1.call-update) | async-done | bytes 4194320 | tf_op jit(solution)/shard_map/all_gather | solution.py:53
  232.1 11.1 %gather_fusion.5 = bf16[128,256,256]{2,1,0:T(8,128)(2,1)} fusion(bf16[32,256,256]{2,1,0:T(8,128)(2,1)} %all-gather.15.cloned.1.call-done, s32[1024]{0:T(1024)S(1)} %pad_clamp_fusion.3), kind=kCustom, calls=%fused_computation.5 | custom fusion | bytes 33554944 | tf_op jit(solution)/shard_map/gather | solution.py:81
  243.2 35.7 %all-gather.9.cloned.1.call-done = bf16[16384,256]{1,0:T(8,128)(2,1)} async-done(((bf16[2048,256]{1,0:T(8,128)(2,1)}), bf16[16384,256]{1,0:T(8,128)(2,1)}) %all-gather.9.cloned.1.call-update) | async-done | bytes 8388624 | tf_op jit(solution)/shard_map/all_gather | solution.py:41
  278.8 5.2 %multiply_reduce_fusion.1 = f32[16384]{0:T(1024)S(1)} fusion(bf16[16384,256]{1,0:T(8,128)(2,1)} %all-gather.9.cloned.1.call-done), kind=kLoop, calls=%fused_computation.34 | loop fusion | flops 12566528 | bytes 8454144 | tf_op jit(solution)/shard_map/reduce_sum | solution.py:16
  284.8 12.8 %gather_fusion.11 = bf16[256,128,256]{2,1,0:T(8,128)(2,1)} fusion(bf16[128,128,256]{2,1,0:T(8,128)(2,1)} %bitcast.128, s32[1024]{0:T(1024)S(1)} %pad_clamp_fusion.1), kind=kCustom, calls=%fused_computation.11 | custom fusion | bytes 33555456 | tf_op jit(solution)/shard_map/gather | solution.py:61
  297.6 14.1 %fusion.16 = f32[128,128,64]{1,2,0:T(8,128)} fusion(bf16[128,256,64]{1,2,0:T(8,128)(2,1)} %gather_fusion.9, bf16[128,256,256]{2,1,0:T(8,128)(2,1)} %gather_fusion.8, bf16[128,128,256]{2,1,0:T(8,128)(2,1)} %bitcast.129, f32[128,256]{1,0:T(8,128)S(1)} %gather_fusion.7, f32[128,128]{1,0:T(8,128)S(1)} %bitcast.135, pred[128]{0:T(512)(128)(4,1)S(1)} %get-tuple-element.6), kind=kOutput, calls=%fused_computation.35 | convolution fusion | flops 2709520384 | bytes 33751168 | tf_op jit(solution)/shard_map/bis,bsw->biw/dot_general | solution.py:28
  311.7 14.3 %fusion.17 = f32[128,128,64]{1,2,0:T(8,128)} fusion(bf16[128,256,64]{1,2,0:T(8,128)(2,1)} %gather_fusion.6, bf16[128,256,256]{2,1,0:T(8,128)(2,1)} %gather_fusion.5, bf16[128,128,256]{2,1,0:T(8,128)(2,1)} %bitcast.130, f32[128,256]{1,0:T(8,128)S(1)} %gather_fusion.4, f32[128,128]{1,0:T(8,128)S(1)} %bitcast.136, pred[128]{0:T(512)(128)(4,1)S(1)} %get-tuple-element.7), kind=kOutput, calls=%fused_computation.36 | convolution fusion | flops 2709520384 | bytes 33751168 | tf_op jit(solution)/shard_map/bis,bsw->biw/dot_general | solution.py:28
  326.0 26.1 %all-gather.11.cloned.1.call-done = bf16[64,256,256]{2,1,0:T(8,128)(2,1)} async-done(((bf16[4,256,256]{2,1,0:T(8,128)(2,1)}), bf16[64,256,256]{2,1,0:T(8,128)(2,1)}) %all-gather.11.cloned.1.call-update) | async-done | bytes 8388624 | tf_op jit(solution)/shard_map/all_gather | solution.py:53
  352.1 5.6 %multiply_reduce_fusion = f32[64,256]{1,0:T(8,128)S(1)} fusion(bf16[64,256,256]{2,1,0:T(8,128)(2,1)} %all-gather.11.cloned.1.call-done), kind=kLoop, calls=%fused_computation.33 | loop fusion | flops 12566528 | bytes 8454144 | tf_op jit(solution)/shard_map/reduce_sum | solution.py:16
  358.5 11.6 %gather_fusion.2 = bf16[128,256,256]{2,1,0:T(8,128)(2,1)} fusion(bf16[64,256,256]{2,1,0:T(8,128)(2,1)} %all-gather.11.cloned.1.call-done, s32[1024]{0:T(1024)S(1)} %pad_clamp_fusion.4), kind=kCustom, calls=%fused_computation.2 | custom fusion | bytes 33554944 | tf_op jit(solution)/shard_map/gather | solution.py:81
  370.1 15.5 %add_bitcast_fusion = f32[128,8,8,128]{3,2,1,0:T(8,128)} fusion(f32[128,128,64]{1,2,0:T(8,128)} %fusion.16, f32[128,128,64]{1,2,0:T(8,128)} %fusion.17, bf16[128,256,64]{1,2,0:T(8,128)(2,1)} %gather_fusion.3, bf16[128,256,256]{2,1,0:T(8,128)(2,1)} %gather_fusion.2, bf16[128,128,256]{2,1,0:T(8,128)(2,1)} %bitcast.131, f32[128,256]{1,0:T(8,128)S(1)} %gather_fusion.1, ...), kind=kOutput, calls=%fused_computation.62 | convolution fusion | flops 2711617536 | bytes 42139776 | tf_op jit(solution)/shard_map/bis,bsw->biw/dot_general | solution.py:28
  385.7 4.5 copy.47
  390.2 12.0 %fusion.87 = bf16[16,128,2048]{1,2,0:T(8,128)(2,1)S(1)} fusion(f32[16,2048]{1,0:T(8,128)S(1)} %add.225, f32[16,128]{1,0:T(8,128)S(1)} %constant_dynamic-slice_fusion, pred[16,2048]{1,0:T(8,128)(4,1)S(1)} %bitcast.143, bf16[16,2048,256]{2,1,0:T(8,128)(2,1)} %bitcast.138, bf16[16,128,256]{2,1,0:T(8,128)(2,1)S(1)} %bitcast.132), kind=kOutput, calls=%fused_computation.17.clone.clone.clone.clone.1 | convolution fusion | flops 2172649472 | bytes 26386432 | tf_op jit(solution)/shard_map/bie,bse->bis/dot_general | solution.py:20
  402.2 5.0 %fusion.43 = f32[16,8,8,128]{3,2,1,0:T(8,128)S(1)} fusion(bf16[16,2048,64]{1,0,2:T(8,128)(2,1)S(1)} %copy-done.2, bf16[16,128,2048]{1,2,0:T(8,128)(2,1)S(1)} %fusion.87), kind=kOutput, calls=%fused_computation.65 | convolution fusion | flops 536870912 | bytes 13107200 | tf_op jit(solution)/shard_map/bis,bsw->biw/dot_general | solution.py:28
  407.2 55.1 %all-reduce.2.cloned.1.call-done = f32[16384,64]{0,1:T(8,128)} async-done(((f32[16384,64]{0,1:T(8,128)}), f32[16384,64]{0,1:T(8,128)}) %all-reduce.2.cloned.1.call-update) | async-done | bytes 4194320 | tf_op jit(solution)/shard_map/psum | solution.py:86
  (66 shorter events, 33.5 us)
Async XLA Ops:
  6.5 10.5 %copy-start.3 = (bf16[7,256,64]{1,2,0:T(8,128)(2,1)S(1)}, bf16[7,256,64]{1,2,0:T(8,128)(2,1)}, u32[]{:S(2)}) copy-start(bf16[7,256,64]{1,2,0:T(8,128)(2,1)} %param.11) | copy-start | bytes 688132
  6.5 13.8 %slice-start = ((bf16[7,256,64]{1,2,0:T(8,128)(2,1)}), bf16[1,256,64]{1,2,0:T(8,128)(2,1)S(1)}, s32[]{:S(2)}) async-start(bf16[7,256,64]{1,2,0:T(8,128)(2,1)} %param.11), calls=%async_computation.8 | async-start | bytes 65536 | tf_op jit(solution)/shard_map/slice | solution.py:54
  6.5 13.5 %copy-start.4 = (s32[16,16]{1,0:T(8,128)S(1)}, s32[16,16]{1,0:T(8,128)}, u32[]{:S(2)}) copy-start(s32[16,16]{1,0:T(8,128)} %param.8) | copy-start | bytes 3076
  6.5 13.8 %copy-start.5 = (s32[128,3,1]{0,2,1:T(1,128)S(1)}, s32[128,3,1]{0,2,1:T(1,128)}, u32[]{:S(2)}) copy-start(s32[128,3,1]{0,2,1:T(1,128)} %param.9) | copy-start | bytes 4612
  6.5 48.4 %all-gather.17.cloned.1.call-start = ((), (), s32[]{:S(2)}) async-start(), calls=%async_computation.4 | async-start | bytes 1114112 | tf_op jit(solution)/shard_map/all_gather | solution.py:54
  8.2 73.2 %all-gather.19.cloned.1.call-start = ((), (), s32[]{:S(2)}) async-start(), calls=%async_computation.6 | async-start | bytes 2359296 | tf_op jit(solution)/shard_map/all_gather | solution.py:42
  8.9 120.0 %all-gather.21.cloned.1.call-start = ((), (), s32[]{:S(2)}) async-start(), calls=%async_computation.7 | async-start | bytes 2228224 | tf_op jit(solution)/shard_map/all_gather | solution.py:53
  17.0 158.2 %all-gather.13.cloned.1.call-start = ((), (), s32[]{:S(2)}) async-start(), calls=%async_computation.2 | async-start | bytes 2228224 | tf_op jit(solution)/shard_map/all_gather | solution.py:54
  17.7 210.3 %all-gather.15.cloned.1.call-start = ((), (), s32[]{:S(2)}) async-start(), calls=%async_computation.3 | async-start | bytes 4456448 | tf_op jit(solution)/shard_map/all_gather | solution.py:53
  18.6 260.3 %all-gather.9.cloned.1.call-start = ((), (), s32[]{:S(2)}) async-start(), calls=%async_computation | async-start | bytes 9437184 | tf_op jit(solution)/shard_map/all_gather | solution.py:41
  19.1 333.0 %all-gather.11.cloned.1.call-start = ((), (), s32[]{:S(2)}) async-start(), calls=%async_computation.1 | async-start | bytes 8912896 | tf_op jit(solution)/shard_map/all_gather | solution.py:53
  20.0 442.3 %all-reduce.2.cloned.1.call-start = ((), (), s32[]{:S(2)}) async-start(), calls=%async_computation.5 | async-start | bytes 8388608 | tf_op jit(solution)/shard_map/psum | solution.py:86
  128.9 10.0 %copy-start = (bf16[4096,256]{1,0:T(8,128)(2,1)S(1)}, bf16[4096,256]{1,0:T(8,128)(2,1)}, u32[]{:S(2)}) copy-start(bf16[4096,256]{1,0:T(8,128)(2,1)} %all-gather.21.cloned.1.call-done) | copy-start | bytes 6291460
  385.7 4.5 copy-start.1
  390.2 12.0 %copy-start.2 = (bf16[16,2048,64]{1,0,2:T(8,128)(2,1)S(1)}, bf16[16,2048,64]{1,0,2:T(8,128)(2,1)}, u32[]{:S(2)}) copy-start(bf16[16,2048,64]{1,0,2:T(8,128)(2,1)} %reshape.311) | copy-start | bytes 12582916
Sparse Core Ops, SparseCore 0:
  9.5 45.4 all-gather.16
  56.6 24.7 all-gather.18
  83.6 45.3 all-gather.20
  130.9 44.2 all-gather.12
  177.2 50.7 all-gather.14
  229.6 49.2 all-gather.8
  281.0 71.0 all-gather.10
  390.3 71.9 all-reduce.1
where the time goes:
time: 472 us; the launch traced here: 471 us
  waiting for transfers between devices  257 us (54%)
  local copies, waits for them, and re-layouts  95.4 us (20%)
  matrix products  60.9 us (13%)
  blocking collectives  26.1 us (6%)
  other arithmetic  17.1 us (4%)
  between operations  13.7 us (3%)
    all_gather x3, waiting for transfers between devices, shards(): lax.all_gather(skel_pts[first_node:last_node], 'tgt', axis=0, tiled=True)  102 us
    psum x1, waiting for transfers between devices, shards(): whole_term = lax.psum(far_total.reshape(row_count, WCOL), 'src')  55.1 us
    dot_general x4, matrix products, apply_tile(): jnp.einsum('bis,bsw->biw', kernel, source_weights, preferred_element_type...  49 us
    all_gather x2, waiting for transfers between devices, shards(): lax.all_gather(equiv_weights[first_node:last_node], 'tgt', axis=0, tiled=...  40.5 us
    all_gather x1, waiting for transfers between devices, shards(): lax.all_gather(points, 'src', axis=0, tiled=True)  35.7 us
    gather x3, local copies, waits for them, and re-layouts, shards(): panel_pts[panel_rows]  32.8 us
    all_gather x1, blocking collectives, shards(): lax.all_gather(equiv_weights[first_node:last_node], 'tgt', axis=0, tiled=...  26.1 us
    all_gather x1, waiting for transfers between devices, shards(): lax.all_gather(weights, 'src', axis=0, tiled=True)  22.5 us
  transfers between devices with their start and end apart: 8, of which 8 were waited for; matrix products, arithmetic and copies ran while one was open for 28% of the time, Pallas kernels for 0%

commit v1 on v0

--- a/solution.py
+++ b/solution.py
@@ -10,6 +10,13 @@
 NEAR = 16
 LEVELS = 3
 kernel_rate = 2.0
+
+
+def swapped_in(block, axis, along):
+    n_dev = lax.axis_size(axis)
+    blocks = jnp.stack([block for _ in range(n_dev)])
+    blocks = lax.all_to_all(blocks, axis, split_axis=0, concat_axis=0)
+    return jnp.concatenate(blocks, axis=along)
 
 
 def square_norms(values):
@@ -38,7 +45,7 @@
     level_nodes = [blk_dev // (4 * 2**tree_level) for tree_level in range(LEVELS)]
     level_start = [sum(level_nodes[:tree_level]) for tree_level in range(LEVELS)]
     group_pts, group_wts = (
-        lax.all_gather(points, "src", axis=0, tiled=True),
+        swapped_in(points, "src", 0),
         lax.all_gather(weights, "src", axis=0, tiled=True),
     )
     tgt_blocks = group_pts.reshape(group_blocks, BLK, E)

time: 472 us -> 426 us (0.903)
  waiting for transfers between devices: 257 us -> 203 us
  starting transfers between devices: 0.32 us -> 5.34 us
    all_gather x1 -> x0, waiting for transfers between devices: 35.7 us -> none  [shards(): lax.all_gather(points, 'src', axis=0, tiled=True)]
    all_gather x3, waiting for transfers between devices: 102 us -> 86.1 us  [shards(): lax.all_gather(skel_pts[first_node:last_node], 'tgt', axis=0, tiled=True)]
    all_gather x2, waiting for transfers between devices: 40.5 us -> 34.9 us  [shards(): lax.all_gather(equiv_weights[first_node:last_node], 'tgt', axis=0, tiled=...]
    all_to_all x0 -> x1, starting transfers between devices: none -> 5.09 us  [swapped_in(): blocks = lax.all_to_all(blocks, axis, split_axis=0, concat_axis=0)]
  transfers between devices with their start and end apart: 8 -> 8, of which waited for: 8 -> 6; matrix products, arithmetic and copies ran while one was open for 28% -> 32% of each run, Pallas kernels for 0% -> 0%
where the time goes in v1:
time: 426 us; the launch traced here: 425 us
  waiting for transfers between devices  203 us (48%)
  local copies, waits for them, and re-layouts  98.4 us (23%)
  matrix products  61.1 us (14%)
  blocking collectives  26.1 us (6%)
  other arithmetic  17.5 us (4%)
  between operations  13.7 us (3%)
  starting transfers between devices  5.34 us (1%)
    all_gather x3, waiting for transfers between devices, shards(): lax.all_gather(skel_pts[first_node:last_node], 'tgt', axis=0, tiled=True)  86.1 us
    psum x1, waiting for transfers between devices, shards(): whole_term = lax.psum(far_total.reshape(row_count, WCOL), 'src')  54.7 us
    dot_general x4, matrix products, apply_tile(): jnp.einsum('bis,bsw->biw', kernel, source_weights, preferred_element_type...  48.8 us
    all_gather x2, waiting for transfers between devices, shards(): lax.all_gather(equiv_weights[first_node:last_node], 'tgt', axis=0, tiled=...  34.9 us
    gather x3, local copies, waits for them, and re-layouts, shards(): panel_pts[panel_rows]  32.1 us
    all_gather x1, waiting for transfers between devices, shards(): lax.all_gather(weights, 'src', axis=0, tiled=True)  26.2 us
    all_gather x1, blocking collectives, shards(): lax.all_gather(equiv_weights[first_node:last_node], 'tgt', axis=0, tiled=...  26.1 us
    reduce_sum x4, other arithmetic, square_norms(): return jnp.sum(jnp.square(values.astype(jnp.float32)), axis=-1)  15.2 us
  transfers between devices with their start and end apart: 8, of which 6 were waited for; matrix products, arithmetic and copies ran while one was open for 32% of the time, Pallas kernels for 0%

profile of v1, /device:TPU:0, one launch (start us, length us, event | category | flops | bytes accessed | tf_op | source)
XLA Modules:
  0.0 424.9 jit_solution(10718558688229748043)
XLA Ops:
  10.4 5.5 %gather_fusion = bf16[1792,256]{1,0:T(8,128)(2,1)S(1)} fusion(bf16[2048,256]{1,0:T(8,128)(2,1)} %param.6, s32[2048]{0:T(1024)S(1)} %pad_clamp_fusion), kind=kCustom, calls=%fused_computation | custom fusion | bytes 1842176 | tf_op jit(solution)/shard_map/jit(_take)/gather | solution.py:54
  23.1 5.1 %all-to-all-start = ((bf16[8,2048,256]{2,1,0:T(8,128)(2,1)}), bf16[8,2048,256]{2,1,0:T(8,128)(2,1)}, u32[]{:S(2)}, u32[]{:S(2)}) async-start(bf16[8,2048,256]{2,1,0:T(8,128)(2,1)} %stack.2), calls=%async_computation | async-start | bytes 16777216 | tf_op jit(solution)/shard_map/all_to_all | solution.py:18
  28.6 26.1 %all_gather.26 = bf16[16,256,64]{1,2,0:T(8,128)(2,1)S(1)} all-gather(bf16[1,256,64]{1,2,0:T(8,128)(2,1)S(1)} %slice-done), channel_id=1, replica_groups=mesh['tgt'=16,'src'=8] {'tgt'}, dimensions={0}, use_global_device_ids=true | all-gather | bytes 557056 | tf_op jit(solution)/shard_map/all_gather | solution.py:61
  61.5 26.2 %all-gather.16.cloned.1.call-done = bf16[16384,64]{0,1:T(8,128)(2,1)} async-done(((bf16[2048,64]{0,1:T(8,128)(2,1)}), bf16[16384,64]{0,1:T(8,128)(2,1)}) %all-gather.16.cloned.1.call-update) | async-done | bytes 2097168 | tf_op jit(solution)/shard_map/all_gather | solution.py:49
  93.0 6.8 %copy.25 = bf16[256,128,64]{1,0,2:T(8,128)(2,1)} copy(bf16[256,128,64]{1,2,0:T(8,128)(2,1)} %gather_fusion.12) | data formatting | bytes 8388608 | tf_op jit(solution)/shard_map/gather | solution.py:70
  99.9 7.3 %reshape.313 = bf16[16,2048,64]{1,0,2:T(8,128)(2,1)} reshape(bf16[256,128,64]{1,0,2:T(8,128)(2,1)} %copy.25) | data formatting | bytes 8388608 | tf_op jit(solution)/shard_map/reshape | solution.py:70
  107.2 27.5 %all-gather.18.cloned.1.call-done = bf16[4096,256]{1,0:T(8,128)(2,1)} async-done(((bf16[256,256]{1,0:T(8,128)(2,1)}), bf16[4096,256]{1,0:T(8,128)(2,1)}) %all-gather.18.cloned.1.call-update) | async-done | bytes 2097168 | tf_op jit(solution)/shard_map/all_gather | solution.py:60
  134.7 10.0 %gather_fusion.8 = bf16[128,256,256]{2,1,0:T(8,128)(2,1)} fusion(bf16[16,256,256]{2,1,0:T(8,128)(2,1)} %bitcast.125, s32[1024]{0:T(1024)S(1)} %pad_clamp_fusion.2), kind=kCustom, calls=%fused_computation.8 | custom fusion | bytes 33554944 | tf_op jit(solution)/shard_map/gather | solution.py:88
  146.1 34.9 %all-gather.10.cloned.1.call-done = bf16[64,256,64]{1,2,0:T(8,128)(2,1)} async-done(((bf16[4,256,64]{1,2,0:T(8,128)(2,1)}), bf16[64,256,64]{1,2,0:T(8,128)(2,1)}) %all-gather.10.cloned.1.call-update) | async-done | bytes 2097168 | tf_op jit(solution)/shard_map/all_gather | solution.py:61
  181.0 4.4 %gather_fusion.3 = bf16[128,256,64]{1,2,0:T(8,128)(2,1)} fusion(bf16[64,256,64]{1,2,0:T(8,128)(2,1)} %all-gather.10.cloned.1.call-done, s32[1024]{0:T(1024)S(1)} %pad_clamp_fusion.4), kind=kCustom, calls=%fused_computation.3 | custom fusion | bytes 8389120 | tf_op jit(solution)/shard_map/gather | solution.py:92
  185.4 5.6 %multiply_reduce_fusion.1 = f32[8,2048]{1,0:T(8,128)S(1)} fusion(bf16[8,2048,256]{2,1,0:T(8,128)(2,1)} %all-to-all-done), kind=kLoop, calls=%fused_computation.34 | loop fusion | flops 12566528 | bytes 8454144 | tf_op jit(solution)/shard_map/reduce_sum | solution.py:23
  191.8 12.9 %gather_fusion.11 = bf16[256,128,256]{2,1,0:T(8,128)(2,1)} fusion(bf16[128,128,256]{2,1,0:T(8,128)(2,1)} %bitcast.4, s32[1024]{0:T(1024)S(1)} %pad_clamp_fusion.1), kind=kCustom, calls=%fused_computation.11 | custom fusion | bytes 33555456 | tf_op jit(solution)/shard_map/gather | solution.py:68
  204.8 14.3 %fusion.16 = f32[128,128,64]{1,2,0:T(8,128)} fusion(bf16[128,256,64]{1,2,0:T(8,128)(2,1)} %gather_fusion.9, bf16[128,256,256]{2,1,0:T(8,128)(2,1)} %gather_fusion.8, bf16[128,128,256]{2,1,0:T(8,128)(2,1)} %bitcast.4, f32[128,256]{1,0:T(8,128)S(1)} %gather_fusion.7, f32[128,128]{1,0:T(8,128)S(1)} %add.200, pred[128]{0:T(512)(128)(4,1)S(1)} %get-tuple-element.6), kind=kOutput, calls=%fused_computation.35 | convolution fusion | flops 2709520384 | bytes 33751168 | tf_op jit(solution)/shard_map/bis,bsw->biw/dot_general | solution.py:35
  219.0 14.7 %all-gather.12.cloned.1.call-done = bf16[32,256,256]{2,1,0:T(8,128)(2,1)} async-done(((bf16[2,256,256]{2,1,0:T(8,128)(2,1)}), bf16[32,256,256]{2,1,0:T(8,128)(2,1)}) %all-gather.12.cloned.1.call-update) | async-done | bytes 4194320 | tf_op jit(solution)/shard_map/all_gather | solution.py:60
  237.9 10.5 %gather_fusion.5 = bf16[128,256,256]{2,1,0:T(8,128)(2,1)} fusion(bf16[32,256,256]{2,1,0:T(8,128)(2,1)} %all-gather.12.cloned.1.call-done, s32[1024]{0:T(1024)S(1)} %pad_clamp_fusion.3), kind=kCustom, calls=%fused_computation.5 | custom fusion | bytes 33554944 | tf_op jit(solution)/shard_map/gather | solution.py:88
  248.4 14.1 %fusion.17 = f32[128,128,64]{1,2,0:T(8,128)} fusion(bf16[128,256,64]{1,2,0:T(8,128)(2,1)} %gather_fusion.6, bf16[128,256,256]{2,1,0:T(8,128)(2,1)} %gather_fusion.5, bf16[128,128,256]{2,1,0:T(8,128)(2,1)} %bitcast.4, f32[128,256]{1,0:T(8,128)S(1)} %gather_fusion.4, f32[128,128]{1,0:T(8,128)S(1)} %add.200, pred[128]{0:T(512)(128)(4,1)S(1)} %get-tuple-element.7), kind=kOutput, calls=%fused_computation.36 | convolution fusion | flops 2709520384 | bytes 33751168 | tf_op jit(solution)/shard_map/bis,bsw->biw/dot_general | solution.py:35
  262.4 43.9 %all-gather.8.cloned.1.call-done = bf16[64,256,256]{2,1,0:T(8,128)(2,1)} async-done(((bf16[4,256,256]{2,1,0:T(8,128)(2,1)}), bf16[64,256,256]{2,1,0:T(8,128)(2,1)}) %all-gather.8.cloned.1.call-update) | async-done | bytes 8388624 | tf_op jit(solution)/shard_map/all_gather | solution.py:60
  306.3 5.6 %multiply_reduce_fusion = f32[64,256]{1,0:T(8,128)S(1)} fusion(bf16[64,256,256]{2,1,0:T(8,128)(2,1)} %all-gather.8.cloned.1.call-done), kind=kLoop, calls=%fused_computation.33 | loop fusion | flops 12566528 | bytes 8454144 | tf_op jit(solution)/shard_map/reduce_sum | solution.py:23
  312.7 11.6 %gather_fusion.2 = bf16[128,256,256]{2,1,0:T(8,128)(2,1)} fusion(bf16[64,256,256]{2,1,0:T(8,128)(2,1)} %all-gather.8.cloned.1.call-done, s32[1024]{0:T(1024)S(1)} %pad_clamp_fusion.4), kind=kCustom, calls=%fused_computation.2 | custom fusion | bytes 33554944 | tf_op jit(solution)/shard_map/gather | solution.py:88
  324.3 15.4 %add_bitcast_fusion = f32[128,8,8,128]{3,2,1,0:T(8,128)} fusion(f32[128,128,64]{1,2,0:T(8,128)} %fusion.16, f32[128,128,64]{1,2,0:T(8,128)} %fusion.17, bf16[128,256,64]{1,2,0:T(8,128)(2,1)} %gather_fusion.3, bf16[128,256,256]{2,1,0:T(8,128)(2,1)} %gather_fusion.2, bf16[128,128,256]{2,1,0:T(8,128)(2,1)} %bitcast.4, f32[128,256]{1,0:T(8,128)S(1)} %gather_fusion.1, ...), kind=kOutput, calls=%fused_computation.62 | convolution fusion | flops 2711617536 | bytes 42139776 | tf_op jit(solution)/shard_map/bis,bsw->biw/dot_general | solution.py:35
  339.8 4.4 %copy.47 = f32[128,8,8,128]{3,2,0,1:T(8,128)} copy(f32[128,8,8,128]{3,2,1,0:T(8,128)} %add_bitcast_fusion) | data formatting | bytes 8388608 | tf_op jit(solution)/shard_map/reshape | solution.py:93
  344.2 12.2 %fusion.87 = bf16[16,128,2048]{1,2,0:T(8,128)(2,1)S(1)} fusion(f32[16,2048]{1,0:T(8,128)S(1)} %add.225, f32[16,128]{1,0:T(8,128)S(1)} %constant_dynamic-slice_fusion, pred[16,2048]{1,0:T(8,128)(4,1)S(1)} %bitcast.133, bf16[16,2048,256]{2,1,0:T(8,128)(2,1)} %bitcast.128, bf16[16,128,256]{2,1,0:T(8,128)(2,1)S(1)} %bitcast.127), kind=kOutput, calls=%fused_computation.17.clone.clone.clone.clone.1 | convolution fusion | flops 2172649472 | bytes 26386432 | tf_op jit(solution)/shard_map/bie,bse->bis/dot_general | solution.py:27
  356.4 5.0 %fusion.43 = f32[16,8,8,128]{3,2,1,0:T(8,128)S(1)} fusion(bf16[16,2048,64]{1,0,2:T(8,128)(2,1)S(1)} %copy-done.2, bf16[16,128,2048]{1,2,0:T(8,128)(2,1)S(1)} %fusion.87), kind=kOutput, calls=%fused_computation.65 | convolution fusion | flops 536870912 | bytes 13107200 | tf_op jit(solution)/shard_map/bis,bsw->biw/dot_general | solution.py:35
  361.5 54.7 %all-reduce.2.cloned.1.call-done = f32[16384,64]{0,1:T(8,128)} async-done(((f32[16384,64]{0,1:T(8,128)}), f32[16384,64]{0,1:T(8,128)}) %all-reduce.2.cloned.1.call-update) | async-done | bytes 4194320 | tf_op jit(solution)/shard_map/psum | solution.py:93
  (67 shorter events, 32.2 us)
Async XLA Ops:
  6.5 10.4 %copy-start.3 = (bf16[7,256,64]{1,2,0:T(8,128)(2,1)S(1)}, bf16[7,256,64]{1,2,0:T(8,128)(2,1)}, u32[]{:S(2)}) copy-start(bf16[7,256,64]{1,2,0:T(8,128)(2,1)} %param.11) | copy-start | bytes 688132
  6.5 12.8 %copy-start.1 = (bf16[2048,256]{1,0:T(8,128)(2,1)S(1)}, bf16[2048,256]{1,0:T(8,128)(2,1)}, u32[]{:S(2)}) copy-start(bf16[2048,256]{1,0:T(8,128)(2,1)} %param.6) | copy-start | bytes 3145732
  6.5 51.0 %all-gather.14.cloned.1.call-start = ((), (), s32[]{:S(2)}) async-start(), calls=%async_computation.4 | async-start | bytes 1114112 | tf_op jit(solution)/shard_map/all_gather | solution.py:61
  8.1 79.6 %all-gather.16.cloned.1.call-start = ((), (), s32[]{:S(2)}) async-start(), calls=%async_computation.6 | async-start | bytes 2359296 | tf_op jit(solution)/shard_map/all_gather | solution.py:49
  8.9 125.8 %all-gather.18.cloned.1.call-start = ((), (), s32[]{:S(2)}) async-start(), calls=%async_computation.7 | async-start | bytes 2228224 | tf_op jit(solution)/shard_map/all_gather | solution.py:60
  16.9 164.1 %all-gather.10.cloned.1.call-start = ((), (), s32[]{:S(2)}) async-start(), calls=%async_computation.2 | async-start | bytes 2228224 | tf_op jit(solution)/shard_map/all_gather | solution.py:61
  17.7 216.1 %all-gather.12.cloned.1.call-start = ((), (), s32[]{:S(2)}) async-start(), calls=%async_computation.3 | async-start | bytes 4456448 | tf_op jit(solution)/shard_map/all_gather | solution.py:60
  18.5 287.9 %all-gather.8.cloned.1.call-start = ((), (), s32[]{:S(2)}) async-start(), calls=%async_computation.1 | async-start | bytes 8912896 | tf_op jit(solution)/shard_map/all_gather | solution.py:60
  23.1 5.2 %copy-start.4 = (s32[16,16]{1,0:T(8,128)S(1)}, s32[16,16]{1,0:T(8,128)}, u32[]{:S(2)}) copy-start(s32[16,16]{1,0:T(8,128)} %param.8) | copy-start | bytes 3076
  23.1 5.4 %copy-start.5 = (s32[128,3,1]{0,2,1:T(1,128)S(1)}, s32[128,3,1]{0,2,1:T(1,128)}, u32[]{:S(2)}) copy-start(s32[128,3,1]{0,2,1:T(1,128)} %param.9) | copy-start | bytes 4612
  23.1 5.5 %slice-start = ((bf16[7,256,64]{1,2,0:T(8,128)(2,1)}), bf16[1,256,64]{1,2,0:T(8,128)(2,1)S(1)}, s32[]{:S(2)}) async-start(bf16[7,256,64]{1,2,0:T(8,128)(2,1)} %param.11), calls=%async_computation.8 | async-start | bytes 65536 | tf_op jit(solution)/shard_map/slice | solution.py:61
  23.1 162.3 %all-to-all-start = ((bf16[8,2048,256]{2,1,0:T(8,128)(2,1)}), bf16[8,2048,256]{2,1,0:T(8,128)(2,1)}, u32[]{:S(2)}, u32[]{:S(2)}) async-start(bf16[8,2048,256]{2,1,0:T(8,128)(2,1)} %stack.2), calls=%async_computation | async-start | bytes 16777216 | tf_op jit(solution)/shard_map/all_to_all | solution.py:18
  28.3 388.0 %all-reduce.2.cloned.1.call-start = ((), (), s32[]{:S(2)}) async-start(), calls=%async_computation.5 | async-start | bytes 8388608 | tf_op jit(solution)/shard_map/psum | solution.py:93
  134.7 10.0 %copy-start = (bf16[4096,256]{1,0:T(8,128)(2,1)S(1)}, bf16[4096,256]{1,0:T(8,128)(2,1)}, u32[]{:S(2)}) copy-start(bf16[4096,256]{1,0:T(8,128)(2,1)} %all-gather.18.cloned.1.call-done) | copy-start | bytes 6291460
  344.2 12.3 %copy-start.2 = (bf16[16,2048,64]{1,0,2:T(8,128)(2,1)S(1)}, bf16[16,2048,64]{1,0,2:T(8,128)(2,1)}, u32[]{:S(2)}) copy-start(bf16[16,2048,64]{1,0,2:T(8,128)(2,1)} %reshape.313) | copy-start | bytes 12582916
Sparse Core Ops, SparseCore 0:
  9.5 45.6 all-gather.13
  56.9 30.7 all-gather.15
  89.8 44.8 all-gather.17
  136.7 44.2 all-gather.9
  183.0 50.7 all-gather.11
  235.8 70.5 all-gather.7
  344.3 71.8 all-reduce.1
